TPU v7x, 32 devices: a whole 2x2x4 slice. The times are simulated.
32 devices in a mesh: tm: 4 (over x, core), rows: 8 (over z, y).
Axes of the slice: x: 2, y: 2, z: 4, core: 2. Of those that a mesh axis runs over, the one named last changes fastest.
Arguments:
- smoother_gains: bfloat16 [4, 1536, 1536], P('tm', 'rows'), may hold values from -1 to 1
- smoother_offsets: bfloat16 [4, 1536], P('tm', 'rows'), may hold values from -6 to 6
- smoother_covs: bfloat16 [4, 1536, 1536], P('tm', 'rows'), may hold values from -1 to 4, as said below
Outputs:
- smoothed_means: bfloat16 [4, 1536], P('tm', 'rows')
- smoothed_covs: bfloat16 [4, 1536, 1536], P('tm', 'rows')
Inputs may be any that keep to these rules, and one draw needn't show every extreme that they name: `smoother_covs`: each step's covariance matrix is symmetric.
All inputs are finite; a program needn't handle non-finite values.
Results may differ from a plain program's by a relative error of at most 0.025.
Values may be sent and summed in bfloat16 or wider, within the bound.
A program may use at most 64 MiB of HBM per device.

v0:
```python
import jax
import jax.numpy as jnp
from jax import lax
from jax.sharding import PartitionSpec as P


def from_behind(block, axis, distance):
    devices = range(lax.axis_size(axis))
    route = [(i - distance, i) for i in devices if i - distance in devices]
    return lax.ppermute(block, axis, route)


def fold_rows(left_panel, pieces):
    return tuple(
        (jnp.dot(left_panel, portion, preferred_element_type=jnp.float32) for portion in pieces)
    )


def shards(smoother_gains, smoother_offsets, smoother_covs):
    own_gain = smoother_gains[0]
    own_offset = smoother_offsets[0]
    own_cov = smoother_covs[0]
    whole_gain = lax.all_gather(own_gain, "rows", axis=0, tiled=True)
    mean_now = own_offset
    cov_now = own_cov
    for round_index in range(lax.axis_size("tm") - 1):
        mean_in, cov_in = from_behind((mean_now, cov_now), "tm", -1)
        mean_sum, left_times = fold_rows(
            own_gain,
            (
                lax.all_gather(mean_in, "rows", axis=0, tiled=True),
                lax.all_gather(cov_in, "rows", axis=0, tiled=True),
            ),
        )
        product_full = lax.dot_general(
            left_times.astype(jnp.bfloat16),
            whole_gain,
            (((1,), (1,)), ((), ())),
            preferred_element_type=jnp.float32,
        )
        mean_now = (mean_sum + own_offset.astype(jnp.float32)).astype(jnp.bfloat16)
        cov_now = (product_full + own_cov.astype(jnp.float32)).astype(jnp.bfloat16)
    return (mean_now[None], cov_now[None])


def solution(mesh):
    in_specs = (P("tm", "rows", None), P("tm", "rows"), P("tm", "rows", None))
    out_specs = (P("tm", "rows"), P("tm", "rows", None))
    return jax.shard_map(shards, mesh=mesh, in_specs=in_specs, out_specs=out_specs, check_vma=False)
```

profile of v0, /device:TPU:0, one launch (start us, length us, event | category | flops | bytes accessed | tf_op | source)
XLA Modules:
  0.0 384.1 jit_solution(2064067778634341476)
XLA Ops:
  7.2 0.7 all-gather.12.cloned.1.call-update
  7.9 1.3 collective-permute-start.3
  9.2 2.8 collective-permute-done.3
  12.1 0.8 copy-done.2
  13.0 79.8 %all-gather.12.cloned.1.call-done = bf16[1,1536,1536]{2,1,0:T(8,128)(2,1)} async-done(((bf16[1,192,1536]{2,1,0:T(8,128)(2,1)}), bf16[1,1536,1536]{2,1,0:T(8,128)(2,1)}) %all-gather.12.cloned.1.call-update) | async-done | bytes 4718608 | tf_op jit(solution)/shard_map/all_gather | solution.py:23
  92.8 80.8 %all-gather.6.cloned.1.call-done = bf16[1536,1536]{1,0:T(8,128)(2,1)} async-done(((bf16[192,1536]{1,0:T(8,128)(2,1)}), bf16[1536,1536]{1,0:T(8,128)(2,1)}) %all-gather.6.cloned.1.call-update) | async-done | bytes 4718608 | tf_op jit(solution)/shard_map/all_gather | solution.py:32
  173.6 6.6 %fusion.15 = bf16[192,1536]{1,0:T(8,128)(2,1)S(1)} fusion(bf16[1,1536,1536]{2,1,0:T(8,128)(2,1)} %all-gather.12.cloned.1.call-done, bf16[1536,1536]{1,0:T(8,128)(2,1)} %all-gather.6.cloned.1.call-done, bf16[1,192,1536]{2,1,0:T(8,128)(2,1)} %param.3, bf16[1,192,1536]{2,1,0:T(8,128)(2,1)} %param.5), kind=kOutput, calls=%fused_computation.12 | convolution fusion | flops 1813118976 | bytes 11206656 | tf_op jit(solution)/shard_map/dot_general | solution.py:35
  180.2 1.3 collective-permute-start.4
  181.5 2.6 collective-permute-done.4
  184.1 0.8 copy-done.3
  185.0 84.1 %all-gather.8.cloned.1.call-done = bf16[1536,1536]{1,0:T(8,128)(2,1)} async-done(((bf16[192,1536]{1,0:T(8,128)(2,1)}), bf16[1536,1536]{1,0:T(8,128)(2,1)}) %all-gather.8.cloned.1.call-update) | async-done | bytes 4718608 | tf_op jit(solution)/shard_map/all_gather | solution.py:32
  269.2 8.8 %fusion.21 = bf16[192,1536]{1,0:T(8,128)(2,1)S(1)} fusion(bf16[1,1536,1536]{2,1,0:T(8,128)(2,1)} %all-gather.12.cloned.1.call-done, bf16[1536,1536]{1,0:T(8,128)(2,1)} %all-gather.8.cloned.1.call-done, bf16[1,192,1536]{2,1,0:T(8,128)(2,1)S(1)} %copy-done, bf16[1,192,1536]{2,1,0:T(8,128)(2,1)S(1)} %copy-done.5), kind=kOutput, calls=%fused_computation.14 | convolution fusion | flops 1813118976 | bytes 11206656 | tf_op jit(solution)/shard_map/dot_general | solution.py:35
  278.0 1.3 collective-permute-start.5
  279.3 2.6 collective-permute-done.5
  281.9 0.8 copy-done.1
  282.7 1.3 collective-permute-start
  284.0 0.6 dynamic-slice
  285.3 7.1 %collective-permute-done = bf16[192]{0:T(256)(128)(2,1)S(1)} collective-permute-done((bf16[192]{0:T(256)(128)(2,1)S(1)}, bf16[192]{0:T(256)(128)(2,1)S(1)}, u32[]{:S(2)}, u32[]{:S(2)}) %collective-permute-start) | collective-permute-done | bytes 416 | tf_op jit(solution)/shard_map/ppermute | solution.py:10
  292.4 0.2 dynamic-update-slice
  292.6 19.1 %all-reduce = bf16[1536]{0:T(1024)(128)(2,1)S(1)} all-reduce(bf16[1536]{0:T(1024)(128)(2,1)S(1)} %dynamic-update-slice), channel_id=1, replica_groups=mesh['tm'=4,'rows'=8] {'rows'}, use_global_device_ids=true, to_apply=%add | all-reduce | flops 1536 | bytes 6144
  311.7 0.2 fusion.37
  312.0 1.3 collective-permute-start.1
  313.3 1.7 collective-permute-done.1
  315.2 17.7 %all-reduce.1 = bf16[1536]{0:T(1024)(128)(2,1)S(1)} all-reduce(bf16[1536]{0:T(1024)(128)(2,1)S(1)} %dynamic-update-slice.1), channel_id=1, replica_groups=mesh['tm'=4,'rows'=8] {'rows'}, use_global_device_ids=true, to_apply=%add.1 | all-reduce | flops 1536 | bytes 6144
  332.9 0.2 fusion.35
  333.1 1.3 collective-permute-start.2
  334.5 1.7 collective-permute-done.2
  336.4 19.7 %all-reduce.2 = bf16[1536]{0:T(1024)(128)(2,1)S(1)} all-reduce(bf16[1536]{0:T(1024)(128)(2,1)S(1)} %dynamic-update-slice.2), channel_id=1, replica_groups=mesh['tm'=4,'rows'=8] {'rows'}, use_global_device_ids=true, to_apply=%add.2 | all-reduce | flops 1536 | bytes 6144
  356.1 0.2 fusion.33
  356.4 0.6 broadcast_in_dim.6
  357.0 11.0 %all-gather.10.cloned.1.call-done = bf16[1536,1536]{1,0:T(8,128)(2,1)} async-done(((bf16[192,1536]{1,0:T(8,128)(2,1)}), bf16[1536,1536]{1,0:T(8,128)(2,1)}) %all-gather.10.cloned.1.call-update) | async-done | bytes 4718608 | tf_op jit(solution)/shard_map/all_gather | solution.py:32
  368.0 9.6 %fusion.24 = bf16[1,192,1536]{2,1,0:T(8,128)(2,1)} fusion(bf16[1,1536,1536]{2,1,0:T(8,128)(2,1)} %all-gather.12.cloned.1.call-done, bf16[1536,1536]{1,0:T(8,128)(2,1)} %all-gather.10.cloned.1.call-done, bf16[1,192,1536]{2,1,0:T(8,128)(2,1)S(1)} %copy-done, bf16[1,192,1536]{2,1,0:T(8,128)(2,1)S(1)} %copy-done.5), kind=kOutput, calls=%fused_computation.15 | convolution fusion | flops 1813118976 | bytes 11206656 | tf_op jit(solution)/shard_map/dot_general | solution.py:35
  (30 shorter events, 0.7 us)
Async XLA Ops:
  7.2 85.6 %all-gather.12.cloned.1.call-start = ((), (), s32[]{:S(2)}) async-start(), calls=%async_computation.3 | async-start | bytes 5308416 | tf_op jit(solution)/shard_map/all_gather | solution.py:23
  7.9 165.7 %all-gather.6.cloned.1.call-start = ((), (), s32[]{:S(2)}) async-start(), calls=%async_computation | async-start | bytes 5308416 | tf_op jit(solution)/shard_map/all_gather | solution.py:32
  7.9 4.1 %collective-permute-start.3 = (bf16[192,1536]{1,0:T(8,128)(2,1)}, bf16[192,1536]{1,0:T(8,128)(2,1)S(1)}, u32[]{:S(2)}, u32[]{:S(2)}) collective-permute-start(bf16[192,1536]{1,0:T(8,128)(2,1)} %bitcast.56), channel_id=1, source_target_pairs={{8,0},{16,8},{24,16},{9,1},{17,9},{25,17},{10,2},{18,10},{26,18},{... | collective-permute-start | bytes 1769480 | tf_op jit(solution)/shard_map/ppermute | solution.py:10
  12.1 0.8 copy-start.2
  12.9 256.3 %copy-start = (bf16[1,192,1536]{2,1,0:T(8,128)(2,1)S(1)}, bf16[1,192,1536]{2,1,0:T(8,128)(2,1)}, u32[]{:S(2)}) copy-start(bf16[1,192,1536]{2,1,0:T(8,128)(2,1)} %param.3) | copy-start | bytes 1769476
  12.9 256.3 %copy-start.5 = (bf16[1,192,1536]{2,1,0:T(8,128)(2,1)S(1)}, bf16[1,192,1536]{2,1,0:T(8,128)(2,1)}, u32[]{:S(2)}) copy-start(bf16[1,192,1536]{2,1,0:T(8,128)(2,1)} %param.5) | copy-start | bytes 1769476
  12.9 256.3 %all-gather.8.cloned.1.call-start = ((), (), s32[]{:S(2)}) async-start(), calls=%async_computation.1 | async-start | bytes 5308416 | tf_op jit(solution)/shard_map/all_gather | solution.py:32
  180.2 3.9 %collective-permute-start.4 = (bf16[192,1536]{1,0:T(8,128)(2,1)S(1)}, bf16[192,1536]{1,0:T(8,128)(2,1)S(1)}, u32[]{:S(2)}, u32[]{:S(2)}) collective-permute-start(bf16[192,1536]{1,0:T(8,128)(2,1)S(1)} %fusion.15), channel_id=1, source_target_pairs={{8,0},{16,8},{24,16},{9,1},{17,9},{25,17},{10,2},{18,10},{26,18},{... | collective-permute-start | bytes 1769480 | tf_op jit(solution)/shard_map/ppermute | solution.py:10
  184.1 0.8 copy-start.3
  185.0 97.7 %copy-start.4 = (bf16[1,192]{1,0:T(2,128)(2,1)S(1)}, bf16[1,192]{1,0:T(2,128)(2,1)}, u32[]{:S(2)}) copy-start(bf16[1,192]{1,0:T(2,128)(2,1)} %param.4) | copy-start | bytes 1156
  185.0 99.1 %copy-start.6 = (u32[32]{0:T(128)S(1)}, u32[32]{0:T(128)}, u32[]{:S(2)}) copy-start(u32[32]{0:T(128)} %constant.5) | copy-start | bytes 388
  185.0 183.0 %all-gather.10.cloned.1.call-start = ((), (), s32[]{:S(2)}) async-start(), calls=%async_computation.2 | async-start | bytes 5308416 | tf_op jit(solution)/shard_map/all_gather | solution.py:32
  278.0 3.9 %collective-permute-start.5 = (bf16[192,1536]{1,0:T(8,128)(2,1)S(1)}, bf16[192,1536]{1,0:T(8,128)(2,1)S(1)}, u32[]{:S(2)}, u32[]{:S(2)}) collective-permute-start(bf16[192,1536]{1,0:T(8,128)(2,1)S(1)} %fusion.21), channel_id=1, source_target_pairs={{8,0},{16,8},{24,16},{9,1},{17,9},{25,17},{10,2},{18,10},{26,18},{... | collective-permute-start | bytes 1769480 | tf_op jit(solution)/shard_map/ppermute | solution.py:10
  281.9 0.8 copy-start.1
  282.7 9.7 %collective-permute-start = (bf16[192]{0:T(256)(128)(2,1)S(1)}, bf16[192]{0:T(256)(128)(2,1)S(1)}, u32[]{:S(2)}, u32[]{:S(2)}) collective-permute-start(bf16[192]{0:T(256)(128)(2,1)S(1)} %reduce), channel_id=1, source_target_pairs={{8,0},{16,8},{24,16},{9,1},{17,9},{25,17},{10,2},{18,10},{26,18},{... | collective-permute-start | bytes 1160 | tf_op jit(solution)/shard_map/ppermute | solution.py:10
  312.0 3.0 collective-permute-start.1
  333.1 3.0 collective-permute-start.2
Sparse Core Ops, SparseCore 0:
  10.2 82.5 all-gather.11
  95.6 78.0 all-gather.5
  185.1 84.0 all-gather.7
  282.8 85.1 all-gather.9
where the time goes:
time: 384 us
  waiting for transfers between devices  275 us (72%)
  blocking collectives  56.6 us (15%)
  matrix products  25.7 us (7%)
  between operations  14.5 us (4%)
  starting transfers between devices  7.96 us (2%)
  local copies, waits for them, and re-layouts  4.25 us (1%)
    all_gather x3, waiting for transfers between devices, shards(): lax.all_gather(cov_in, 'rows', axis=0, tiled=True)  176 us
    all_gather x1, waiting for transfers between devices, shards(): whole_gain = lax.all_gather(own_gain, 'rows', axis=0, tiled=True)  79.8 us
    unnamed x3, blocking collectives  56.6 us
    dot_general x3, matrix products, shards(): lax.dot_general(left_times.astype(jnp.bfloat16), whole_gain, (((1,), (1,)...  25 us
    ppermute x6, waiting for transfers between devices, from_behind(): return lax.ppermute(block, axis, route)  18.6 us
    ppermute x6, starting transfers between devices, from_behind(): return lax.ppermute(block, axis, route)  7.8 us
  transfers between devices with their start and end apart: 10, of which 10 were waited for; matrix products, arithmetic and copies ran while one was open for 1% of the time, Pallas kernels for 0%

commit v1 on v0

--- a/solution.py
+++ b/solution.py
@@ -1,7 +1,27 @@
+import functools
 import jax
 import jax.numpy as jnp
 from jax import lax
 from jax.sharding import PartitionSpec as P
+
+
+def choose_corner_here(arr_in, named_axis):
+    world = lax.axis_size(named_axis)
+    blocks_here = tuple(((it, (it + 1) % world) for it in range(world)))
+    cards = tuple(((it, (it - 1) % world) for it in range(world)))
+    carry_out, work_now = ([arr_in], [arr_in])
+    for _ in range(world // 2):
+        plain = lax.ppermute(carry_out[-1], named_axis, blocks_here)
+        carry_out.append(plain)
+    for _ in range((world - 1) // 2):
+        aux = lax.ppermute(work_now[-1], named_axis, cards)
+        work_now.append(aux)
+    t1 = jnp.concatenate([*carry_out[::-1], *work_now[1:]], axis=0)
+    arr_now = lax.axis_index(named_axis)
+    return jnp.roll(t1, (arr_now - world // 2) * arr_in.shape[0], axis=0)
+
+
+see_the_chains = functools.partial(choose_corner_here, named_axis="rows")
 
 
 def from_behind(block, axis, distance):
@@ -26,11 +46,7 @@
     for round_index in range(lax.axis_size("tm") - 1):
         mean_in, cov_in = from_behind((mean_now, cov_now), "tm", -1)
         mean_sum, left_times = fold_rows(
-            own_gain,
-            (
-                lax.all_gather(mean_in, "rows", axis=0, tiled=True),
-                lax.all_gather(cov_in, "rows", axis=0, tiled=True),
-            ),
+            own_gain, (lax.all_gather(mean_in, "rows", axis=0, tiled=True), see_the_chains(cov_in))
         )
         product_full = lax.dot_general(
             left_times.astype(jnp.bfloat16),

time: 384 us -> 444 us (1.16)
  starting transfers between devices: 7.96 us -> 59.4 us
  waiting for transfers between devices: 275 us -> 233 us
  local copies, waits for them, and re-layouts: 4.25 us -> 27 us
  blocking collectives: 56.6 us -> 77.6 us
  matrix products: 25.7 us -> 31.4 us
    all_gather x3 -> x0, waiting for transfers between devices: 176 us -> none  [shards(): lax.all_gather(cov_in, 'rows', axis=0, tiled=True)]
    ppermute x0 -> x21, waiting for transfers between devices: none -> 176 us  [the longest x12 127 us: choose_corner_here(): plain = lax.ppermute(carry_out[-1], named_axis, blocks_here)]
    all_gather x1, waiting for transfers between devices: 79.8 us -> 17.3 us  [shards(): whole_gain = lax.all_gather(own_gain, 'rows', axis=0, tiled=True)]
    ppermute x0 -> x21, starting transfers between devices: none -> 51.4 us  [the longest x9 32.8 us: choose_corner_here(): aux = lax.ppermute(work_now[-1], named_axis, cards)]
    unnamed x3, blocking collectives: 56.6 us -> 77.6 us
    ppermute x6, waiting for transfers between devices: 18.6 us -> 39.2 us  [from_behind(): return lax.ppermute(block, axis, route)]
    unnamed x24 -> x39, local copies, waits for them, and re-layouts: 3.64 us -> 23.8 us
    dot_general x3, matrix products: 25 us -> 30.7 us  [shards(): lax.dot_general(left_times.astype(jnp.bfloat16), whole_gain, (((1,), (1,)...]
  transfers between devices with their start and end apart: 10 -> 28, of which waited for: 10 -> 18; matrix products, arithmetic and copies ran while one was open for 1% -> 6% of each run, Pallas kernels for 0% -> 0%
where the time goes in v1:
time: 444 us; the launch traced here: 443 us
  waiting for transfers between devices  233 us (52%)
  blocking collectives  77.6 us (17%)
  starting transfers between devices  59.4 us (13%)
  matrix products  31.4 us (7%)
  local copies, waits for them, and re-layouts  27 us (6%)
  between operations  14.8 us (3%)
    ppermute x12, waiting for transfers between devices, choose_corner_here(): plain = lax.ppermute(carry_out[-1], named_axis, blocks_here)  127 us
    unnamed x3, blocking collectives  77.6 us
    ppermute x9, waiting for transfers between devices, choose_corner_here(): aux = lax.ppermute(work_now[-1], named_axis, cards)  48.6 us
    ppermute x6, waiting for transfers between devices, from_behind(): return lax.ppermute(block, axis, route)  39.2 us
    ppermute x9, starting transfers between devices, choose_corner_here(): aux = lax.ppermute(work_now[-1], named_axis, cards)  32.8 us
    dot_general x3, matrix products, shards(): lax.dot_general(left_times.astype(jnp.bfloat16), whole_gain, (((1,), (1,)...  30.7 us
    unnamed x39, local copies, waits for them, and re-layouts  23.8 us
    ppermute x12, starting transfers between devices, choose_corner_here(): plain = lax.ppermute(carry_out[-1], named_axis, blocks_here)  18.6 us
  transfers between devices with their start and end apart: 28, of which 18 were waited for; matrix products, arithmetic and copies ran while one was open for 6% of the time, Pallas kernels for 0%

profile of v1, /device:TPU:0, one launch (start us, length us, event | category | flops | bytes accessed | tf_op | source)
XLA Modules:
  0.0 443.3 jit_solution(7127490120876023505)
XLA Ops:
  9.2 2.8 collective-permute-done.3
  12.0 3.0 collective-permute-start.4
  15.0 11.1 %collective-permute-done.4 = bf16[192,1536]{1,0:T(8,128)(2,1)S(1)} collective-permute-done((bf16[192,1536]{1,0:T(8,128)(2,1)S(1)}, bf16[192,1536]{1,0:T(8,128)(2,1)S(1)}, u32[]{:S(2)}, u32[]{:S(2)}) %collective-permute-start.4) | collective-permute-done | bytes 589856 | tf_op jit(solution)/shard_map/ppermute | solution.py:14
  26.9 3.8 collective-permute-start.8
  30.8 25.0 %collective-permute-done.5 = bf16[192,1536]{1,0:T(8,128)(2,1)S(1)} collective-permute-done((bf16[192,1536]{1,0:T(8,128)(2,1)S(1)}, bf16[192,1536]{1,0:T(8,128)(2,1)S(1)}, u32[]{:S(2)}, u32[]{:S(2)}) %collective-permute-start.5) | collective-permute-done | bytes 589856 | tf_op jit(solution)/shard_map/ppermute | solution.py:14
  55.7 4.7 %collective-permute-start.9 = (bf16[192,1536]{1,0:T(8,128)(2,1)S(1)}, bf16[192,1536]{1,0:T(8,128)(2,1)S(1)}, u32[]{:S(2)}, u32[]{:S(2)}) collective-permute-start(bf16[192,1536]{1,0:T(8,128)(2,1)S(1)} %collective-permute-done.8), channel_id=1, source_target_pairs={{0,7},{1,0},{2,1},{3,2},{4,3},{5,4},{6,5},{7,6},{8,15},{9,8},{10,9... | collective-permute-start | bytes 1769480 | tf_op jit(solution)/shard_map/ppermute | solution.py:17
  60.5 30.8 %collective-permute-done.6 = bf16[192,1536]{1,0:T(8,128)(2,1)} collective-permute-done((bf16[192,1536]{1,0:T(8,128)(2,1)S(1)}, bf16[192,1536]{1,0:T(8,128)(2,1)}, u32[]{:S(2)}, u32[]{:S(2)}) %collective-permute-start.6) | collective-permute-done | bytes 589856 | tf_op jit(solution)/shard_map/ppermute | solution.py:14
  91.3 2.6 collective-permute-start.7
  93.8 17.1 %collective-permute-start.10 = (bf16[192,1536]{1,0:T(8,128)(2,1)S(1)}, bf16[192,1536]{1,0:T(8,128)(2,1)S(1)}, u32[]{:S(2)}, u32[]{:S(2)}) collective-permute-start(bf16[192,1536]{1,0:T(8,128)(2,1)S(1)} %collective-permute-done.9), channel_id=1, source_target_pairs={{0,7},{1,0},{2,1},{3,2},{4,3},{5,4},{6,5},{7,6},{8,15},{9,8},{10,9... | collective-permute-start | bytes 1769480 | tf_op jit(solution)/shard_map/ppermute | solution.py:17
  110.9 18.3 %collective-permute-done.7 = bf16[192,1536]{1,0:T(8,128)(2,1)} collective-permute-done((bf16[192,1536]{1,0:T(8,128)(2,1)}, bf16[192,1536]{1,0:T(8,128)(2,1)}, u32[]{:S(2)}, u32[]{:S(2)}) %collective-permute-start.7) | collective-permute-done | bytes 589856 | tf_op jit(solution)/shard_map/ppermute | solution.py:14
  138.4 17.3 %all-gather.3.cloned.1.call-done = bf16[1,1536,1536]{2,1,0:T(8,128)(2,1)} async-done(((bf16[1,192,1536]{2,1,0:T(8,128)(2,1)}), bf16[1,1536,1536]{2,1,0:T(8,128)(2,1)}) %all-gather.3.cloned.1.call-update) | async-done | bytes 4718608 | tf_op jit(solution)/shard_map/all_gather | solution.py:43
  155.7 10.0 %fusion.39 = bf16[192,1536]{1,0:T(8,128)(2,1)S(1)} fusion(bf16[1,1536,1536]{2,1,0:T(8,128)(2,1)} %all-gather.3.cloned.1.call-done, s32[]{:T(128)S(6)} %select_n.15, bf16[1536,1536]{1,0:T(8,128)(2,1)} %constant_dynamic-update-slice_fusion, bf16[1,192,1536]{2,1,0:T(8,128)(2,1)S(1)} %copy-done, bf16[1,192,1536]{2,1,0:T(8,128)(2,1)} %param.7), kind=kOutput, calls=%fused_computation.26 | convolution fusion | flops 1822556160 | bytes 11206660 | tf_op jit(solution)/shard_map/dot_general | solution.py:51
  167.1 9.2 %collective-permute-done.11 = bf16[192,1536]{1,0:T(8,128)(2,1)S(1)} collective-permute-done((bf16[192,1536]{1,0:T(8,128)(2,1)S(1)}, bf16[192,1536]{1,0:T(8,128)(2,1)S(1)}, u32[]{:S(2)}, u32[]{:S(2)}) %collective-permute-start.11) | collective-permute-done | bytes 589856 | tf_op jit(solution)/shard_map/ppermute | solution.py:30
  176.3 12.6 %collective-permute-done.12 = bf16[192,1536]{1,0:T(8,128)(2,1)S(1)} collective-permute-done((bf16[192,1536]{1,0:T(8,128)(2,1)S(1)}, bf16[192,1536]{1,0:T(8,128)(2,1)S(1)}, u32[]{:S(2)}, u32[]{:S(2)}) %collective-permute-start.12) | collective-permute-done | bytes 589856 | tf_op jit(solution)/shard_map/ppermute | solution.py:14
  188.9 4.7 %collective-permute-start.16 = (bf16[192,1536]{1,0:T(8,128)(2,1)S(1)}, bf16[192,1536]{1,0:T(8,128)(2,1)S(1)}, u32[]{:S(2)}, u32[]{:S(2)}) collective-permute-start(bf16[192,1536]{1,0:T(8,128)(2,1)S(1)} %collective-permute-done.11), channel_id=1, source_target_pairs={{0,7},{1,0},{2,1},{3,2},{4,3},{5,4},{6,5},{7,6},{8,15},{9,8},{10,9... | collective-permute-start | bytes 1769480 | tf_op jit(solution)/shard_map/ppermute | solution.py:17
  193.6 17.1 %collective-permute-done.13 = bf16[192,1536]{1,0:T(8,128)(2,1)S(1)} collective-permute-done((bf16[192,1536]{1,0:T(8,128)(2,1)S(1)}, bf16[192,1536]{1,0:T(8,128)(2,1)S(1)}, u32[]{:S(2)}, u32[]{:S(2)}) %collective-permute-start.13) | collective-permute-done | bytes 589856 | tf_op jit(solution)/shard_map/ppermute | solution.py:14
  210.7 2.6 collective-permute-start.14
  213.3 11.4 %collective-permute-done.16 = bf16[192,1536]{1,0:T(8,128)(2,1)S(1)} collective-permute-done((bf16[192,1536]{1,0:T(8,128)(2,1)S(1)}, bf16[192,1536]{1,0:T(8,128)(2,1)S(1)}, u32[]{:S(2)}, u32[]{:S(2)}) %collective-permute-start.16) | collective-permute-done | bytes 589856 | tf_op jit(solution)/shard_map/ppermute | solution.py:17
  224.8 2.1 collective-permute-start.15
  226.8 28.3 %collective-permute-done.17 = bf16[192,1536]{1,0:T(8,128)(2,1)S(1)} collective-permute-done((bf16[192,1536]{1,0:T(8,128)(2,1)S(1)}, bf16[192,1536]{1,0:T(8,128)(2,1)S(1)}, u32[]{:S(2)}, u32[]{:S(2)}) %collective-permute-start.17) | collective-permute-done | bytes 589856 | tf_op jit(solution)/shard_map/ppermute | solution.py:17
  261.3 7.4 %collective-permute-done.18 = bf16[192,1536]{1,0:T(8,128)(2,1)S(1)} collective-permute-done((bf16[192,1536]{1,0:T(8,128)(2,1)S(1)}, bf16[192,1536]{1,0:T(8,128)(2,1)S(1)}, u32[]{:S(2)}, u32[]{:S(2)}) %collective-permute-start.18) | collective-permute-done | bytes 589856 | tf_op jit(solution)/shard_map/ppermute | solution.py:17
  269.6 9.9 %fusion.36 = bf16[192,1536]{1,0:T(8,128)(2,1)S(1)} fusion(bf16[1,1536,1536]{2,1,0:T(8,128)(2,1)} %all-gather.3.cloned.1.call-done, s32[]{:T(128)S(6)} %select_n.15, bf16[1536,1536]{1,0:T(8,128)(2,1)} %constant_dynamic-update-slice_fusion.8, bf16[1,192,1536]{2,1,0:T(8,128)(2,1)S(1)} %copy-done, bf16[1,192,1536]{2,1,0:T(8,128)(2,1)S(1)} %copy-done.2), kind=kOutput, calls=%fused_computation.25 | convolution fusion | flops 1822556160 | bytes 11206660 | tf_op jit(solution)/shard_map/dot_general | solution.py:51
  280.8 5.1 %collective-permute-done.19 = bf16[192,1536]{1,0:T(8,128)(2,1)S(1)} collective-permute-done((bf16[192,1536]{1,0:T(8,128)(2,1)S(1)}, bf16[192,1536]{1,0:T(8,128)(2,1)S(1)}, u32[]{:S(2)}, u32[]{:S(2)}) %collective-permute-start.19) | collective-permute-done | bytes 589856 | tf_op jit(solution)/shard_map/ppermute | solution.py:30
  286.1 12.4 %collective-permute-done.20 = bf16[192,1536]{1,0:T(8,128)(2,1)S(1)} collective-permute-done((bf16[192,1536]{1,0:T(8,128)(2,1)S(1)}, bf16[192,1536]{1,0:T(8,128)(2,1)S(1)}, u32[]{:S(2)}, u32[]{:S(2)}) %collective-permute-start.20) | collective-permute-done | bytes 589856 | tf_op jit(solution)/shard_map/ppermute | solution.py:14
  301.1 18.7 %collective-permute-done = bf16[192]{0:T(256)(128)(2,1)S(1)} collective-permute-done((bf16[192]{0:T(256)(128)(2,1)S(1)}, bf16[192]{0:T(256)(128)(2,1)S(1)}, u32[]{:S(2)}, u32[]{:S(2)}) %collective-permute-start) | collective-permute-done | bytes 416 | tf_op jit(solution)/shard_map/ppermute | solution.py:30
  319.9 21.5 %all-reduce = bf16[1536]{0:T(1024)(128)(2,1)S(1)} all-reduce(bf16[1536]{0:T(1024)(128)(2,1)S(1)} %dynamic-update-slice), channel_id=1, replica_groups=mesh['tm'=4,'rows'=8] {'rows'}, use_global_device_ids=true, to_apply=%add | all-reduce | flops 1536 | bytes 6144
  341.6 2.0 collective-permute-start.22
  347.0 30.9 %all-reduce.1 = bf16[1536]{0:T(1024)(128)(2,1)S(1)} all-reduce(bf16[1536]{0:T(1024)(128)(2,1)S(1)} %dynamic-update-slice.1), channel_id=1, replica_groups=mesh['tm'=4,'rows'=8] {'rows'}, use_global_device_ids=true, to_apply=%add.1 | all-reduce | flops 1536 | bytes 6144
  378.2 2.0 collective-permute-start.25
  380.2 5.3 %collective-permute-start.23 = (bf16[192,1536]{1,0:T(8,128)(2,1)S(1)}, bf16[192,1536]{1,0:T(8,128)(2,1)}, u32[]{:S(2)}, u32[]{:S(2)}) collective-permute-start(bf16[192,1536]{1,0:T(8,128)(2,1)S(1)} %collective-permute-done.22), channel_id=1, source_target_pairs={{0,1},{1,2},{2,3},{3,4},{4,5},{5,6},{6,7},{7,0},{8,9},{9,10},{10,1... | collective-permute-start | bytes 1769480 | tf_op jit(solution)/shard_map/ppermute | solution.py:14
  388.7 25.2 %all-reduce.2 = bf16[1536]{0:T(1024)(128)(2,1)S(1)} all-reduce(bf16[1536]{0:T(1024)(128)(2,1)S(1)} %dynamic-update-slice.2), channel_id=1, replica_groups=mesh['tm'=4,'rows'=8] {'rows'}, use_global_device_ids=true, to_apply=%add.2 | all-reduce | flops 1536 | bytes 6144
  425.7 10.8 %fusion.42 = bf16[1,192,1536]{2,1,0:T(8,128)(2,1)} fusion(bf16[1,1536,1536]{2,1,0:T(8,128)(2,1)} %all-gather.3.cloned.1.call-done, s32[]{:T(128)S(6)} %select_n.15, bf16[1536,1536]{1,0:T(8,128)(2,1)} %constant_dynamic-update-slice_fusion.16, bf16[1,192,1536]{2,1,0:T(8,128)(2,1)S(1)} %copy-done, bf16[1,192,1536]{2,1,0:T(8,128)(2,1)} %param.7), kind=kOutput, calls=%fused_computation.27 | convolution fusion | flops 1822556160 | bytes 11206660 | tf_op jit(solution)/shard_map/dot_general | solution.py:51
  (81 shorter events, 42.9 us)
Async XLA Ops:
  7.2 148.6 %all-gather.3.cloned.1.call-start = ((), (), s32[]{:S(2)}) async-start(), calls=%async_computation | async-start | bytes 5308416 | tf_op jit(solution)/shard_map/all_gather | solution.py:43
  7.9 4.1 collective-permute-start.3
  12.0 14.0 %collective-permute-start.4 = (bf16[192,1536]{1,0:T(8,128)(2,1)S(1)}, bf16[192,1536]{1,0:T(8,128)(2,1)S(1)}, u32[]{:S(2)}, u32[]{:S(2)}) collective-permute-start(bf16[192,1536]{1,0:T(8,128)(2,1)S(1)} %collective-permute-done.3), channel_id=1, source_target_pairs={{0,1},{1,2},{2,3},{3,4},{4,5},{5,6},{6,7},{7,0},{8,9},{9,10},{10,1... | collective-permute-start | bytes 1769480 | tf_op jit(solution)/shard_map/ppermute | solution.py:14
  26.0 29.7 %collective-permute-start.5 = (bf16[192,1536]{1,0:T(8,128)(2,1)S(1)}, bf16[192,1536]{1,0:T(8,128)(2,1)S(1)}, u32[]{:S(2)}, u32[]{:S(2)}) collective-permute-start(bf16[192,1536]{1,0:T(8,128)(2,1)S(1)} %collective-permute-done.4), channel_id=1, source_target_pairs={{0,1},{1,2},{2,3},{3,4},{4,5},{5,6},{6,7},{7,0},{8,9},{9,10},{10,1... | collective-permute-start | bytes 1769480 | tf_op jit(solution)/shard_map/ppermute | solution.py:14
  26.9 28.8 %collective-permute-start.8 = (bf16[192,1536]{1,0:T(8,128)(2,1)S(1)}, bf16[192,1536]{1,0:T(8,128)(2,1)S(1)}, u32[]{:S(2)}, u32[]{:S(2)}) collective-permute-start(bf16[192,1536]{1,0:T(8,128)(2,1)S(1)} %collective-permute-done.3), channel_id=1, source_target_pairs={{0,7},{1,0},{2,1},{3,2},{4,3},{5,4},{6,5},{7,6},{8,15},{9,8},{10,9... | collective-permute-start | bytes 1769480 | tf_op jit(solution)/shard_map/ppermute | solution.py:17
  55.7 35.5 %collective-permute-start.6 = (bf16[192,1536]{1,0:T(8,128)(2,1)S(1)}, bf16[192,1536]{1,0:T(8,128)(2,1)}, u32[]{:S(2)}, u32[]{:S(2)}) collective-permute-start(bf16[192,1536]{1,0:T(8,128)(2,1)S(1)} %collective-permute-done.5), channel_id=1, source_target_pairs={{0,1},{1,2},{2,3},{3,4},{4,5},{5,6},{6,7},{7,0},{8,9},{9,10},{10,1... | collective-permute-start | bytes 1769480 | tf_op jit(solution)/shard_map/ppermute | solution.py:14
  55.7 38.1 %collective-permute-start.9 = (bf16[192,1536]{1,0:T(8,128)(2,1)S(1)}, bf16[192,1536]{1,0:T(8,128)(2,1)S(1)}, u32[]{:S(2)}, u32[]{:S(2)}) collective-permute-start(bf16[192,1536]{1,0:T(8,128)(2,1)S(1)} %collective-permute-done.8), channel_id=1, source_target_pairs={{0,7},{1,0},{2,1},{3,2},{4,3},{5,4},{6,5},{7,6},{8,15},{9,8},{10,9... | collective-permute-start | bytes 1769480 | tf_op jit(solution)/shard_map/ppermute | solution.py:17
  91.3 38.0 %collective-permute-start.7 = (bf16[192,1536]{1,0:T(8,128)(2,1)}, bf16[192,1536]{1,0:T(8,128)(2,1)}, u32[]{:S(2)}, u32[]{:S(2)}) collective-permute-start(bf16[192,1536]{1,0:T(8,128)(2,1)} %collective-permute-done.6), channel_id=1, source_target_pairs={{0,1},{1,2},{2,3},{3,4},{4,5},{5,6},{6,7},{7,0},{8,9},{9,10},{10,1... | collective-permute-start | bytes 1769480 | tf_op jit(solution)/shard_map/ppermute | solution.py:14
  93.8 61.9 %copy-start = (bf16[1,192,1536]{2,1,0:T(8,128)(2,1)S(1)}, bf16[1,192,1536]{2,1,0:T(8,128)(2,1)}, u32[]{:S(2)}) copy-start(bf16[1,192,1536]{2,1,0:T(8,128)(2,1)} %param.5) | copy-start | bytes 1769476
  93.8 43.7 %collective-permute-start.10 = (bf16[192,1536]{1,0:T(8,128)(2,1)S(1)}, bf16[192,1536]{1,0:T(8,128)(2,1)S(1)}, u32[]{:S(2)}, u32[]{:S(2)}) collective-permute-start(bf16[192,1536]{1,0:T(8,128)(2,1)S(1)} %collective-permute-done.9), channel_id=1, source_target_pairs={{0,7},{1,0},{2,1},{3,2},{4,3},{5,4},{6,5},{7,6},{8,15},{9,8},{10,9... | collective-permute-start | bytes 1769480 | tf_op jit(solution)/shard_map/ppermute | solution.py:17
  165.7 103.9 %copy-start.2 = (bf16[1,192,1536]{2,1,0:T(8,128)(2,1)S(1)}, bf16[1,192,1536]{2,1,0:T(8,128)(2,1)}, u32[]{:S(2)}) copy-start(bf16[1,192,1536]{2,1,0:T(8,128)(2,1)} %param.7) | copy-start | bytes 1769476
  165.7 10.6 %collective-permute-start.11 = (bf16[192,1536]{1,0:T(8,128)(2,1)S(1)}, bf16[192,1536]{1,0:T(8,128)(2,1)S(1)}, u32[]{:S(2)}, u32[]{:S(2)}) collective-permute-start(bf16[192,1536]{1,0:T(8,128)(2,1)S(1)} %fusion.39), channel_id=1, source_target_pairs={{8,0},{16,8},{24,16},{9,1},{17,9},{25,17},{10,2},{18,10},{26,18},{... | collective-permute-start | bytes 1769480 | tf_op jit(solution)/shard_map/ppermute | solution.py:30
  176.3 12.6 %collective-permute-start.12 = (bf16[192,1536]{1,0:T(8,128)(2,1)S(1)}, bf16[192,1536]{1,0:T(8,128)(2,1)S(1)}, u32[]{:S(2)}, u32[]{:S(2)}) collective-permute-start(bf16[192,1536]{1,0:T(8,128)(2,1)S(1)} %collective-permute-done.11), channel_id=1, source_target_pairs={{0,1},{1,2},{2,3},{3,4},{4,5},{5,6},{6,7},{7,0},{8,9},{9,10},{10,1... | collective-permute-start | bytes 1769480 | tf_op jit(solution)/shard_map/ppermute | solution.py:14
  188.9 21.8 %collective-permute-start.13 = (bf16[192,1536]{1,0:T(8,128)(2,1)S(1)}, bf16[192,1536]{1,0:T(8,128)(2,1)S(1)}, u32[]{:S(2)}, u32[]{:S(2)}) collective-permute-start(bf16[192,1536]{1,0:T(8,128)(2,1)S(1)} %collective-permute-done.12), channel_id=1, source_target_pairs={{0,1},{1,2},{2,3},{3,4},{4,5},{5,6},{6,7},{7,0},{8,9},{9,10},{10,1... | collective-permute-start | bytes 1769480 | tf_op jit(solution)/shard_map/ppermute | solution.py:14
  188.9 35.9 %collective-permute-start.16 = (bf16[192,1536]{1,0:T(8,128)(2,1)S(1)}, bf16[192,1536]{1,0:T(8,128)(2,1)S(1)}, u32[]{:S(2)}, u32[]{:S(2)}) collective-permute-start(bf16[192,1536]{1,0:T(8,128)(2,1)S(1)} %collective-permute-done.11), channel_id=1, source_target_pairs={{0,7},{1,0},{2,1},{3,2},{4,3},{5,4},{6,5},{7,6},{8,15},{9,8},{10,9... | collective-permute-start | bytes 1769480 | tf_op jit(solution)/shard_map/ppermute | solution.py:17
  210.7 14.1 %collective-permute-start.14 = (bf16[192,1536]{1,0:T(8,128)(2,1)S(1)}, bf16[192,1536]{1,0:T(8,128)(2,1)S(1)}, u32[]{:S(2)}, u32[]{:S(2)}) collective-permute-start(bf16[192,1536]{1,0:T(8,128)(2,1)S(1)} %collective-permute-done.13), channel_id=1, source_target_pairs={{0,1},{1,2},{2,3},{3,4},{4,5},{5,6},{6,7},{7,0},{8,9},{9,10},{10,1... | collective-permute-start | bytes 1769480 | tf_op jit(solution)/shard_map/ppermute | solution.py:14
  224.8 30.4 %collective-permute-start.17 = (bf16[192,1536]{1,0:T(8,128)(2,1)S(1)}, bf16[192,1536]{1,0:T(8,128)(2,1)S(1)}, u32[]{:S(2)}, u32[]{:S(2)}) collective-permute-start(bf16[192,1536]{1,0:T(8,128)(2,1)S(1)} %collective-permute-done.16), channel_id=1, source_target_pairs={{0,7},{1,0},{2,1},{3,2},{4,3},{5,4},{6,5},{7,6},{8,15},{9,8},{10,9... | collective-permute-start | bytes 1769480 | tf_op jit(solution)/shard_map/ppermute | solution.py:17
  224.8 30.4 %collective-permute-start.15 = (bf16[192,1536]{1,0:T(8,128)(2,1)S(1)}, bf16[192,1536]{1,0:T(8,128)(2,1)S(1)}, u32[]{:S(2)}, u32[]{:S(2)}) collective-permute-start(bf16[192,1536]{1,0:T(8,128)(2,1)S(1)} %collective-permute-done.14), channel_id=1, source_target_pairs={{0,1},{1,2},{2,3},{3,4},{4,5},{5,6},{6,7},{7,0},{8,9},{9,10},{10,1... | collective-permute-start | bytes 1769480 | tf_op jit(solution)/shard_map/ppermute | solution.py:14
  255.2 13.5 %collective-permute-start.18 = (bf16[192,1536]{1,0:T(8,128)(2,1)S(1)}, bf16[192,1536]{1,0:T(8,128)(2,1)S(1)}, u32[]{:S(2)}, u32[]{:S(2)}) collective-permute-start(bf16[192,1536]{1,0:T(8,128)(2,1)S(1)} %collective-permute-done.17), channel_id=1, source_target_pairs={{0,7},{1,0},{2,1},{3,2},{4,3},{5,4},{6,5},{7,6},{8,15},{9,8},{10,9... | collective-permute-start | bytes 1769480 | tf_op jit(solution)/shard_map/ppermute | solution.py:17
  269.6 28.9 %copy-start.1 = (bf16[1,192]{1,0:T(2,128)(2,1)S(1)}, bf16[1,192]{1,0:T(2,128)(2,1)}, u32[]{:S(2)}) copy-start(bf16[1,192]{1,0:T(2,128)(2,1)} %param.6) | copy-start | bytes 1156
  269.6 30.3 %copy-start.3 = (u32[32]{0:T(128)S(1)}, u32[32]{0:T(128)}, u32[]{:S(2)}) copy-start(u32[32]{0:T(128)} %constant.28) | copy-start | bytes 388
  279.5 6.4 %collective-permute-start.19 = (bf16[192,1536]{1,0:T(8,128)(2,1)S(1)}, bf16[192,1536]{1,0:T(8,128)(2,1)S(1)}, u32[]{:S(2)}, u32[]{:S(2)}) collective-permute-start(bf16[192,1536]{1,0:T(8,128)(2,1)S(1)} %fusion.36), channel_id=1, source_target_pairs={{8,0},{16,8},{24,16},{9,1},{17,9},{25,17},{10,2},{18,10},{26,18},{... | collective-permute-start | bytes 1769480 | tf_op jit(solution)/shard_map/ppermute | solution.py:30
  285.9 12.6 %collective-permute-start.20 = (bf16[192,1536]{1,0:T(8,128)(2,1)S(1)}, bf16[192,1536]{1,0:T(8,128)(2,1)S(1)}, u32[]{:S(2)}, u32[]{:S(2)}) collective-permute-start(bf16[192,1536]{1,0:T(8,128)(2,1)S(1)} %collective-permute-done.19), channel_id=1, source_target_pairs={{0,1},{1,2},{2,3},{3,4},{4,5},{5,6},{6,7},{7,0},{8,9},{9,10},{10,1... | collective-permute-start | bytes 1769480 | tf_op jit(solution)/shard_map/ppermute | solution.py:14
  298.5 43.1 %collective-permute-start.21 = (bf16[192,1536]{1,0:T(8,128)(2,1)S(1)}, bf16[192,1536]{1,0:T(8,128)(2,1)S(1)}, u32[]{:S(2)}, u32[]{:S(2)}) collective-permute-start(bf16[192,1536]{1,0:T(8,128)(2,1)S(1)} %collective-permute-done.20), channel_id=1, source_target_pairs={{0,1},{1,2},{2,3},{3,4},{4,5},{5,6},{6,7},{7,0},{8,9},{9,10},{10,1... | collective-permute-start | bytes 1769480 | tf_op jit(solution)/shard_map/ppermute | solution.py:14
  298.5 21.2 %collective-permute-start = (bf16[192]{0:T(256)(128)(2,1)S(1)}, bf16[192]{0:T(256)(128)(2,1)S(1)}, u32[]{:S(2)}, u32[]{:S(2)}) collective-permute-start(bf16[192]{0:T(256)(128)(2,1)S(1)} %reduce), channel_id=1, source_target_pairs={{8,0},{16,8},{24,16},{9,1},{17,9},{25,17},{10,2},{18,10},{26,18},{... | collective-permute-start | bytes 1160 | tf_op jit(solution)/shard_map/ppermute | solution.py:30
  341.5 36.7 %collective-permute-start.24 = (bf16[192,1536]{1,0:T(8,128)(2,1)S(1)}, bf16[192,1536]{1,0:T(8,128)(2,1)S(1)}, u32[]{:S(2)}, u32[]{:S(2)}) collective-permute-start(bf16[192,1536]{1,0:T(8,128)(2,1)S(1)} %collective-permute-done.19), channel_id=1, source_target_pairs={{0,7},{1,0},{2,1},{3,2},{4,3},{5,4},{6,5},{7,6},{8,15},{9,8},{10,9... | collective-permute-start | bytes 1769480 | tf_op jit(solution)/shard_map/ppermute | solution.py:17
  341.6 38.6 %collective-permute-start.22 = (bf16[192,1536]{1,0:T(8,128)(2,1)S(1)}, bf16[192,1536]{1,0:T(8,128)(2,1)S(1)}, u32[]{:S(2)}, u32[]{:S(2)}) collective-permute-start(bf16[192,1536]{1,0:T(8,128)(2,1)S(1)} %collective-permute-done.21), channel_id=1, source_target_pairs={{0,1},{1,2},{2,3},{3,4},{4,5},{5,6},{6,7},{7,0},{8,9},{9,10},{10,1... | collective-permute-start | bytes 1769480 | tf_op jit(solution)/shard_map/ppermute | solution.py:14
  343.8 3.0 collective-permute-start.1
  378.2 36.5 %collective-permute-start.25 = (bf16[192,1536]{1,0:T(8,128)(2,1)S(1)}, bf16[192,1536]{1,0:T(8,128)(2,1)}, u32[]{:S(2)}, u32[]{:S(2)}) collective-permute-start(bf16[192,1536]{1,0:T(8,128)(2,1)S(1)} %collective-permute-done.24), channel_id=1, source_target_pairs={{0,7},{1,0},{2,1},{3,2},{4,3},{5,4},{6,5},{7,6},{8,15},{9,8},{10,9... | collective-permute-start | bytes 1769480 | tf_op jit(solution)/shard_map/ppermute | solution.py:17
  380.2 34.9 %collective-permute-start.23 = (bf16[192,1536]{1,0:T(8,128)(2,1)S(1)}, bf16[192,1536]{1,0:T(8,128)(2,1)}, u32[]{:S(2)}, u32[]{:S(2)}) collective-permute-start(bf16[192,1536]{1,0:T(8,128)(2,1)S(1)} %collective-permute-done.22), channel_id=1, source_target_pairs={{0,1},{1,2},{2,3},{3,4},{4,5},{5,6},{6,7},{7,0},{8,9},{9,10},{10,1... | collective-permute-start | bytes 1769480 | tf_op jit(solution)/shard_map/ppermute | solution.py:14
  385.5 3.0 collective-permute-start.2
  414.7 10.1 %collective-permute-start.26 = (bf16[192,1536]{1,0:T(8,128)(2,1)}, bf16[192,1536]{1,0:T(8,128)(2,1)S(1)}, u32[]{:S(2)}, u32[]{:S(2)}) collective-permute-start(bf16[192,1536]{1,0:T(8,128)(2,1)} %collective-permute-done.25), channel_id=1, source_target_pairs={{0,7},{1,0},{2,1},{3,2},{4,3},{5,4},{6,5},{7,6},{8,15},{9,8},{10,9... | collective-permute-start | bytes 1769480 | tf_op jit(solution)/shard_map/ppermute | solution.py:17
Sparse Core Ops, SparseCore 0:
  10.2 145.4 all-gather.2
